TPU v7x, 32 devices: a whole 2x2x4 slice. The times are simulated.
32 devices in a mesh: groups: 2 (over x), ctx: 16 (over z, y, core).
Axes of the slice: x: 2, y: 2, z: 4, core: 2. Of those that a mesh axis runs over, the one named last changes fastest.
Arguments:
- context_keys: bfloat16 [4096, 2048], P(('groups', 'ctx')), parts along dimension 0, may hold values from -6 to 6
- context_values: bfloat16 [4096, 2048], P(('groups', 'ctx')), parts along dimension 0, may hold values from -6 to 6
- context_queries: bfloat16 [4096, 2048], P(('groups', 'ctx')), parts along dimension 0, may hold values from -6 to 6
- token_rates: float32 [8, 4096], P(None, ('groups', 'ctx')), parts along dimension 1, may hold values from 0.05 to 1
- w_gate: bfloat16 [8, 256, 256], replicated, may hold values from -0.375 to 0.375
- w_up: bfloat16 [8, 256, 256], replicated, may hold values from -0.375 to 0.375
- w_down: bfloat16 [8, 256, 256], replicated, may hold values from -0.375 to 0.375
- question_rows: bfloat16 [8192, 2048], P(('groups', 'ctx')), parts along dimension 0, may hold values from -6 to 6
- question_count: int32 [32], P(('groups', 'ctx')), parts along dimension 0, may hold values from 1 to 256, 1024 in all
Outputs:
- context_out: bfloat16 [4096, 2048], P(('groups', 'ctx')), parts along dimension 0
- answers: bfloat16 [8192, 2048], P(('groups', 'ctx')), parts along dimension 0
There are 2 independent parts, one for each index of `groups`. A program takes and returns all parts, laid end to end along the dimension named above; an argument that names none is the same for every part. Nothing has to cross between parts.
Inputs may be any that keep to these rules, and one draw needn't show every extreme that they name: `question_count`: live rows are the first of each device's 256 slots. The counts of one user (the devices along ctx) add up to exactly 1024, and some device of each user has exactly 256.
All inputs are finite; a program needn't handle non-finite values.
Results may differ from a plain program's by a relative error of at most 0.018.
Values may be sent and summed in bfloat16 or wider, within the bound.
A program may use at most 128 MiB of HBM per device.

v0:
```python
import jax
import jax.numpy as jnp
from jax import lax
from jax.sharding import PartitionSpec as P

NS_STEPS = 3
quintic_first = 3.4445
quintic_second = -4.775
quintic_third = 2.0315


def fast_apply(in_rows, w_gate, w_up, w_down):
    head_count = w_gate.shape[0]
    head_size = w_gate.shape[1]
    row_split = in_rows.reshape(in_rows.shape[0], head_count, head_size)
    pre_gate = jnp.einsum("thd,hde->hte", row_split, w_gate, preferred_element_type=jnp.float32)
    pre_up = jnp.einsum("thd,hde->hte", row_split, w_up, preferred_element_type=jnp.float32)
    hidden = (jax.nn.silu(pre_gate) * pre_up).astype(jnp.bfloat16)
    outputs = jnp.einsum("hte,hef->thf", hidden, w_down, preferred_element_type=jnp.float32)
    return outputs.reshape(in_rows.shape[0], head_count * head_size).astype(jnp.bfloat16)


def directions(context_keys, context_values, token_rates, w_gate, w_up, w_down):
    tok_rows = context_keys.shape[0]
    head_count = w_gate.shape[0]
    head_size = w_gate.shape[1]
    key_split = context_keys.reshape(tok_rows, head_count, head_size)
    value_split = context_values.reshape(tok_rows, head_count, head_size)
    pre_gate = jnp.einsum("thd,hde->hte", key_split, w_gate, preferred_element_type=jnp.float32)
    pre_up = jnp.einsum("thd,hde->hte", key_split, w_up, preferred_element_type=jnp.float32)
    sigmoid_gate = jax.nn.sigmoid(pre_gate)
    activated = pre_gate * sigmoid_gate
    hidden = (activated * pre_up).astype(jnp.bfloat16)
    weighted = (token_rates.T[:, :, None] * value_split).astype(jnp.bfloat16)
    back_hidden = jnp.einsum("thf,hef->hte", weighted, w_down, preferred_element_type=jnp.float32)
    back_gate = (
        back_hidden * pre_up * sigmoid_gate * (1.0 + pre_gate * (1.0 - sigmoid_gate))
    ).astype(jnp.bfloat16)
    back_up = (back_hidden * activated).astype(jnp.bfloat16)
    step_gate = jnp.einsum("thd,hte->hde", key_split, back_gate, preferred_element_type=jnp.float32)
    step_up = jnp.einsum("thd,hte->hde", key_split, back_up, preferred_element_type=jnp.float32)
    step_down = jnp.einsum("hte,thf->hef", hidden, weighted, preferred_element_type=jnp.float32)
    return jnp.stack([step_gate, step_up, step_down])


def per_device(
    context_keys,
    context_values,
    context_queries,
    token_rates,
    w_gate,
    w_up,
    w_down,
    question_rows,
    question_count,
):
    head_count = w_gate.shape[0]
    head_size = w_gate.shape[1]
    matrix_count = 3 * head_count
    context_out = fast_apply(context_queries, w_gate, w_up, w_down)
    direction = directions(context_keys, context_values, token_rates, w_gate, w_up, w_down)
    flat_grads = direction.reshape(matrix_count, head_size * head_size)
    total = lax.psum(flat_grads, "ctx")
    norm_sizes = jnp.sqrt(jnp.sum(total * total, axis=1, keepdims=True))
    scaled = (total / (norm_sizes + 1e-06)).astype(jnp.bfloat16)
    iterate = scaled.reshape(matrix_count, head_size, head_size)
    for sweep_index in range(NS_STEPS):
        gram_matrix = jnp.einsum(
            "mij,mkj->mik", iterate, iterate, preferred_element_type=jnp.float32
        ).astype(jnp.bfloat16)
        gram_square = jnp.einsum(
            "mij,mjk->mik", gram_matrix, gram_matrix, preferred_element_type=jnp.float32
        )
        polynomial = (
            quintic_second * gram_matrix.astype(jnp.float32) + quintic_third * gram_square
        ).astype(jnp.bfloat16)
        product = jnp.einsum(
            "mij,mjk->mik", polynomial, iterate, preferred_element_type=jnp.float32
        )
        iterate = (quintic_first * iterate.astype(jnp.float32) + product).astype(jnp.bfloat16)
    previous = jnp.stack([w_gate, w_up, w_down]).astype(jnp.float32)
    moved = previous + iterate.reshape(3, head_count, head_size, head_size).astype(jnp.float32)
    col_norms = jnp.sqrt(jnp.sum(previous * previous, axis=2, keepdims=True))
    updated = (
        moved * col_norms / jnp.sqrt(jnp.sum(moved * moved, axis=2, keepdims=True) + 1e-06)
    ).astype(jnp.bfloat16)
    capacity = question_rows.shape[0]
    outputs = fast_apply(question_rows, updated[0], updated[1], updated[2])
    live_mask = jnp.arange(capacity, dtype=jnp.int32) < question_count[0]
    answers = jnp.where(live_mask[:, None], outputs, jnp.zeros_like(outputs))
    return (context_out, answers)


def solution(mesh):
    return jax.shard_map(
        per_device,
        mesh=mesh,
        in_specs=(
            P(("groups", "ctx"), None),
            P(("groups", "ctx"), None),
            P(("groups", "ctx"), None),
            P(None, ("groups", "ctx")),
            P(),
            P(),
            P(),
            P(("groups", "ctx"), None),
            P(("groups", "ctx")),
        ),
        out_specs=(P(("groups", "ctx"), None), P(("groups", "ctx"), None)),
        check_vma=False,
    )
```

profile of v0, /device:TPU:0, one launch (start us, length us, event | category | flops | bytes accessed | tf_op | source)
XLA Modules:
  0.0 236.1 jit_solution(8442899116746412055)
XLA Ops:
  7.2 0.0 copy-start.11
  7.2 0.0 copy-start.16
  7.2 0.0 all-reduce.2.cloned.1.call-start
  7.2 0.0 copy-start.9
  7.2 0.0 copy-start.17
  7.3 1.8 fusion.41
  9.1 0.0 copy-done.11
  9.1 1.4 fusion.43
  10.5 0.0 copy-done.16
  10.5 0.1 convert_element_type.148
  10.6 0.0 copy-done.9
  10.6 0.0 copy-done.17
  10.6 0.5 fusion.61
  11.1 0.0 copy-start.15
  11.1 0.7 convolution_bitcast_fusion
  11.8 0.4 copy-done.15
  12.1 0.6 convolution_bitcast_fusion.2
  12.8 0.6 convolution_bitcast_fusion.1
  13.4 3.3 %pad_maximum_fusion = f32[3,8,256,256]{2,3,1,0:T(8,128)} fusion(f32[1,8,256,256]{2,3,1,0:T(8,128)S(1)} %convolution_bitcast_fusion, f32[1,8,256,256]{2,3,1,0:T(8,128)S(1)} %convolution_bitcast_fusion.1, f32[1,8,256,256]{2,3,1,0:T(8,128)S(1)} %convolution_bitcast_fusion.2), kind=kLoop, calls=%fused_computation | loop fusion | flops 3145728 | bytes 12582912 | tf_op jit(solution)/shard_map/stack | solution.py:43
  16.7 6.7 %copy.60 = f32[3,8,256,256]{3,1,2,0:T(8,128)} copy(f32[3,8,256,256]{2,3,1,0:T(8,128)} %pad_maximum_fusion) | data formatting | bytes 12582912
  23.4 0.0 all-reduce.2.cloned.1.call-update
  23.4 1.2 copy-done.7
  24.6 0.5 copy.31
  25.1 0.0 copy-start.1
  25.1 0.5 copy.32
  25.6 0.0 copy-start.3
  25.7 1.9 copy.33
  27.5 0.0 copy-start.5
  27.5 3.1 %maximum_convert_fusion = f32[3,8,256,256]{2,3,1,0:T(8,128)} fusion(bf16[1,8,256,256]{2,3,1,0:T(8,128)(2,1)S(1)} %bitcast.124, bf16[1,8,256,256]{2,3,1,0:T(8,128)(2,1)S(1)} %bitcast.121, bf16[1,8,256,256]{2,3,1,0:T(8,128)(2,1)S(1)} %bitcast.118), kind=kLoop, calls=%fused_computation.18 | loop fusion | flops 4718592 | bytes 9437184 | tf_op jit(solution)/shard_map/convert_element_type | solution.py:81
  30.6 7.0 %copy.45 = f32[3,8,256,256]{3,2,1,0:T(8,128)} copy(f32[3,8,256,256]{2,3,1,0:T(8,128)} %maximum_convert_fusion) | data formatting | bytes 12582912 | tf_op jit(solution)/shard_map/convert_element_type | solution.py:81
  37.6 0.0 copy-done.1
  37.6 0.0 copy-done.3
  37.6 0.0 copy-done.5
  37.6 1.0 multiply_reduce_fusion
  38.6 0.0 copy-start.10
  38.6 0.0 copy-start.12
  38.6 2.4 %copy.56 = bf16[256,2048]{0,1:T(8,128)(2,1)} copy(bf16[256,2048]{1,0:T(8,128)(2,1)} %param.16) | data formatting | bytes 2097152 | tf_op jit(solution)/shard_map/reshape | solution.py:15
  41.7 1.7 fusion.47
  43.4 0.0 copy-done.10
  43.4 0.0 copy-done.12
  43.4 2.5 %fusion.29 = bf16[128,8,256]{2,0,1:T(8,128)(2,1)} fusion(bf16[8,256,256]{2,1,0:T(8,128)(2,1)S(1)} %copy-done.10, bf16[8,256,256]{2,1,0:T(8,128)(2,1)S(1)} %copy-done.12, f32[8,128,256]{2,1,0:T(8,128)S(1)} %fusion.47, bf16[16,8,8,256]{3,2,1,0:T(8,128)(2,1)} %bitcast.140), kind=kOutput, calls=%fused_computation.45 | convolution fusion | flops 270270464 | bytes 4194304 | tf_op jit(solution)/shard_map/hte,hef->thf/dot_general | solution.py:19
  45.9 1.3 copy.30
  47.2 1.0 copy.49
  48.3 117.3 %all-reduce.2.cloned.1.call-done = f32[24,65536]{1,0:T(8,128)} async-done(((f32[24,65536]{1,0:T(8,128)}), f32[24,65536]{1,0:T(8,128)}) %all-reduce.2.cloned.1.call-update) | async-done | bytes 6291472 | tf_op jit(solution)/shard_map/psum | solution.py:63
  165.5 3.6 %multiply_reduce_fusion.1 = f32[24]{0:T(128)S(1)} fusion(f32[24,65536]{1,0:T(8,128)} %all-reduce.2.cloned.1.call-done), kind=kLoop, calls=%fused_computation.13 | loop fusion | flops 3145704 | bytes 6291552 | tf_op jit(solution)/shard_map/reduce_sum | solution.py:64
  169.1 1.0 copy-done
  170.1 0.4 divide_convert_fusion.1
  170.5 0.7 copy.61
  171.3 2.7 %fusion.74 = bf16[24,256,256]{2,1,0:T(8,128)(2,1)} fusion(bf16[24,256,256]{2,1,0:T(8,128)(2,1)S(1)} %bitcast.115), kind=kOutput, calls=%fused_computation.96 | convolution fusion | flops 805306368 | bytes 6291456 | tf_op jit(solution)/shard_map/mij,mkj->mik/dot_general | solution.py:68
  173.9 7.8 %add_convert_fusion.4 = bf16[24,256,256]{2,1,0:T(8,128)(2,1)} fusion(bf16[24,256,256]{2,1,0:T(8,128)(2,1)S(1)} %bitcast.116, bf16[24,256,256]{2,1,0:T(8,128)(2,1)} %fusion.74), kind=kOutput, calls=%fused_computation.10 | convolution fusion | flops 1624768512 | bytes 9437184 | tf_op jit(solution)/shard_map/mij,mjk->mik/dot_general | solution.py:77
  181.8 5.5 %fusion.75 = bf16[24,256,256]{2,1,0:T(8,128)(2,1)} fusion(bf16[24,256,256]{2,1,0:T(8,128)(2,1)} %add_convert_fusion.4), kind=kOutput, calls=%fused_computation.97 | convolution fusion | flops 805306368 | bytes 6291456 | tf_op jit(solution)/shard_map/mij,mkj->mik/dot_general | solution.py:68
  187.3 8.2 %add_convert_fusion.2 = bf16[24,256,256]{2,1,0:T(8,128)(2,1)S(1)} fusion(bf16[24,256,256]{2,1,0:T(8,128)(2,1)} %add_convert_fusion.4, bf16[24,256,256]{2,1,0:T(8,128)(2,1)} %fusion.75), kind=kOutput, calls=%fused_computation.8 | convolution fusion | flops 1624768512 | bytes 9437184 | tf_op jit(solution)/shard_map/mij,mjk->mik/dot_general | solution.py:77
  195.5 2.7 %fusion.76 = bf16[24,256,256]{2,1,0:T(8,128)(2,1)} fusion(bf16[24,256,256]{2,1,0:T(8,128)(2,1)S(1)} %add_convert_fusion.2), kind=kOutput, calls=%fused_computation.98 | convolution fusion | flops 805306368 | bytes 6291456 | tf_op jit(solution)/shard_map/mij,mkj->mik/dot_general | solution.py:68
  198.1 11.6 %fusion.1 = (f32[24,256]{1,0:T(8,128)S(1)}, f32[24,256,256]{2,1,0:T(8,128)}) fusion(f32[3,8,256,256]{3,2,1,0:T(8,128)} %copy.45, bf16[24,256,256]{2,1,0:T(8,128)(2,1)S(1)} %add_convert_fusion.2, bf16[24,256,256]{2,1,0:T(8,128)(2,1)} %fusion.76), kind=kOutput, calls=%fused_computation.3 | convolution fusion | flops 1631053824 | bytes 18898944 | tf_op jit(solution)/shard_map/mij,mjk->mik/dot_general | solution.py:77
  209.7 6.7 %copy.44 = f32[3,8,256,256]{2,3,1,0:T(8,128)} copy(f32[3,8,256,256]{3,2,1,0:T(8,128)} %bitcast.128) | data formatting | bytes 12582912 | tf_op jit(solution)/shard_map/convert_element_type | solution.py:82
  216.5 0.0 copy-start.13
  216.5 4.6 %divide_convert_fusion = bf16[3,8,256,256]{2,3,1,0:T(8,128)(2,1)S(1)} fusion(f32[3,8,256,256]{2,3,1,0:T(8,128)} %copy.44, f32[3,8,256]{2,1,0:T(8,128)S(1)} %sqrt_bitcast_fusion, f32[3,8,256]{2,1,0:T(8,128)S(1)} %sqrt.28, bf16[1,8,256,256]{2,3,1,0:T(8,128)(2,1)S(1)} %bitcast.126, bf16[1,8,256,256]{2,3,1,0:T(8,128)(2,1)S(1)} %bitcast.123, ...), kind=kLoop, calls=%fused_computation.4 | loop fusion | flops 11010048 | bytes 12632064 | tf_op jit(solution)/shard_map/convert_element_type | solution.py:86
  221.1 0.0 copy-start.14
  221.1 1.6 copy-done.8
  222.7 0.4 fusion.31
  223.1 0.0 copy-done.14
  223.1 3.5 %convolution_convert_fusion = bf16[8,256,256]{2,1,0:T(8,128)(2,1)} fusion(f32[8,256,256]{2,1,0:T(8,128)S(1)} %fusion.31, bf16[256,8,256]{0,2,1:T(8,128)(2,1)S(1)} %bitcast.132, bf16[3,8,256,256]{2,3,1,0:T(8,128)(2,1)} %copy-done.8), kind=kOutput, calls=%fused_computation.41 | convolution fusion | flops 540540928 | bytes 6291456 | tf_op jit(solution)/shard_map/hte,hef->thf/dot_general | solution.py:19
  226.7 1.5 copy.48
  228.2 1.1 broadcast_select_fusion
  (14 shorter events, 0.1 us)
Async XLA Ops:
  7.2 1.9 copy-start.11
  7.2 3.3 %copy-start.16 = (bf16[128,2048]{1,0:T(8,128)(2,1)S(1)}, bf16[128,2048]{1,0:T(8,128)(2,1)}, u32[]{:S(2)}) copy-start(bf16[128,2048]{1,0:T(8,128)(2,1)} %param.10) | copy-start | bytes 1572868
  7.2 158.3 %all-reduce.2.cloned.1.call-start = ((), (), s32[]{:S(2)}) async-start(), calls=%async_computation | async-start | bytes 12582912 | tf_op jit(solution)/shard_map/psum | solution.py:63
  7.2 3.4 %copy-start.9 = (bf16[8,256,256]{2,1,0:T(8,128)(2,1)S(1)}, bf16[8,256,256]{2,1,0:T(8,128)(2,1)}, u32[]{:S(2)}) copy-start(bf16[8,256,256]{2,1,0:T(8,128)(2,1)} %param.15) | copy-start | bytes 3145732
  7.2 3.3 %copy-start.17 = (f32[8,128]{1,0:T(8,128)S(1)}, f32[8,128]{1,0:T(8,128)}, u32[]{:S(2)}) copy-start(f32[8,128]{1,0:T(8,128)} %param.12) | copy-start | bytes 12292
  11.1 1.0 copy-start.15
  23.4 1.2 copy-start.7
  25.1 12.5 %copy-start.1 = (bf16[8,256,256]{1,2,0:T(8,128)(2,1)}, bf16[8,256,256]{1,2,0:T(8,128)(2,1)S(1)}, u32[]{:S(2)}) copy-start(bf16[8,256,256]{1,2,0:T(8,128)(2,1)S(1)} %copy.31) | copy-start | bytes 3145732
  25.6 11.9 %copy-start.3 = (bf16[8,256,256]{1,2,0:T(8,128)(2,1)}, bf16[8,256,256]{1,2,0:T(8,128)(2,1)S(1)}, u32[]{:S(2)}) copy-start(bf16[8,256,256]{1,2,0:T(8,128)(2,1)S(1)} %copy.32) | copy-start | bytes 3145732
  27.5 10.1 %copy-start.5 = (bf16[8,256,256]{1,2,0:T(8,128)(2,1)}, bf16[8,256,256]{1,2,0:T(8,128)(2,1)S(1)}, u32[]{:S(2)}) copy-start(bf16[8,256,256]{1,2,0:T(8,128)(2,1)S(1)} %copy.33) | copy-start | bytes 3145732
  38.6 4.8 %copy-start.10 = (bf16[8,256,256]{2,1,0:T(8,128)(2,1)S(1)}, bf16[8,256,256]{2,1,0:T(8,128)(2,1)}, u32[]{:S(2)}) copy-start(bf16[8,256,256]{2,1,0:T(8,128)(2,1)} %param.15) | copy-start | bytes 3145732
  38.6 4.8 %copy-start.12 = (bf16[8,256,256]{2,1,0:T(8,128)(2,1)S(1)}, bf16[8,256,256]{2,1,0:T(8,128)(2,1)}, u32[]{:S(2)}) copy-start(bf16[8,256,256]{2,1,0:T(8,128)(2,1)} %param.14) | copy-start | bytes 3145732
  165.5 4.6 %copy-start = (f32[24,65536]{1,0:T(8,128)S(1)}, f32[24,65536]{1,0:T(8,128)}, u32[]{:S(2)}) copy-start(f32[24,65536]{1,0:T(8,128)} %all-reduce.2.cloned.1.call-done) | copy-start | bytes 18874372
  209.7 6.7 %copy-start.2 = (bf16[8,256,256]{1,2,0:T(8,128)(2,1)S(1)}, bf16[8,256,256]{1,2,0:T(8,128)(2,1)}, u32[]{:S(2)}) copy-start(bf16[8,256,256]{1,2,0:T(8,128)(2,1)} %copy-done.1) | copy-start | bytes 3145732
  209.7 6.7 %copy-start.4 = (bf16[8,256,256]{1,2,0:T(8,128)(2,1)S(1)}, bf16[8,256,256]{1,2,0:T(8,128)(2,1)}, u32[]{:S(2)}) copy-start(bf16[8,256,256]{1,2,0:T(8,128)(2,1)} %copy-done.3) | copy-start | bytes 3145732
  209.7 6.7 %copy-start.6 = (bf16[8,256,256]{1,2,0:T(8,128)(2,1)S(1)}, bf16[8,256,256]{1,2,0:T(8,128)(2,1)}, u32[]{:S(2)}) copy-start(bf16[8,256,256]{1,2,0:T(8,128)(2,1)} %copy-done.5) | copy-start | bytes 3145732
  216.5 6.2 %copy-start.13 = (bf16[256,2048]{0,1:T(8,128)(2,1)S(1)}, bf16[256,2048]{0,1:T(8,128)(2,1)}, u32[]{:S(2)}) copy-start(bf16[256,2048]{0,1:T(8,128)(2,1)} %copy.56) | copy-start | bytes 3145732
  221.1 1.6 copy-start.8
  221.1 2.1 copy-start.14
Sparse Core Ops, SparseCore 0:
  23.5 141.9 all-reduce.1
where the time goes:
time: 237 us; the launch traced here: 236 us
  waiting for transfers between devices  117 us (49%)
  matrix products  52.2 us (22%)
  local copies, waits for them, and re-layouts  34.4 us (15%)
  other arithmetic  17.2 us (7%)
  between operations  15 us (6%)
    psum x1, waiting for transfers between devices, per_device(): total = lax.psum(flat_grads, 'ctx')  117 us
    dot_general x3, matrix products, per_device(): jnp.einsum('mij,mjk->mik', polynomial, iterate, preferred_element_type=jn...  27.6 us
    unnamed x42, local copies, waits for them, and re-layouts  15.6 us
    dot_general x3, matrix products, per_device(): jnp.einsum('mij,mkj->mik', iterate, iterate, preferred_element_type=jnp.f...  10.9 us
    convert_element_type x1, local copies, waits for them, and re-layouts, per_device(): previous = jnp.stack([w_gate, w_up, w_down]).astype(jnp.float32)  6.96 us
    convert_element_type x1, local copies, waits for them, and re-layouts, per_device(): iterate.reshape(3, head_count, head_size, head_size).astype(jnp.float32)  6.7 us
    dot_general x2, matrix products, fast_apply(): jnp.einsum('hte,hef->thf', hidden, w_down, preferred_element_type=jnp.flo...  6.01 us
  transfers between devices with their start and end apart: 1, of which 1 were waited for; matrix products, arithmetic and copies ran while one was open for 10% of the time, Pallas kernels for 0%

commit v1 on v0

--- a/solution.py
+++ b/solution.py
@@ -1,12 +1,26 @@
+import functools
 import jax
 import jax.numpy as jnp
 from jax import lax
 from jax.sharding import PartitionSpec as P
+from jax.lax import axis_size, ppermute
 
 NS_STEPS = 3
 quintic_first = 3.4445
 quintic_second = -4.775
 quintic_third = 2.0315
+
+
+def boxes_name(inner_x, mesh_ax):
+    axis_total = axis_size(mesh_ax)
+    side_arr = inner_x
+    plain = lambda vec_out: [(hop_no, hop_no ^ vec_out) for hop_no in range(axis_total)]
+    for dev_j in range(axis_total.bit_length() - 1):
+        side_arr = side_arr + ppermute(side_arr, mesh_ax, plain(1 << dev_j))
+    return side_arr
+
+
+attach_leaves = functools.partial(boxes_name, mesh_ax="ctx")
 
 
 def fast_apply(in_rows, w_gate, w_up, w_down):
@@ -60,7 +74,7 @@
     context_out = fast_apply(context_queries, w_gate, w_up, w_down)
     direction = directions(context_keys, context_values, token_rates, w_gate, w_up, w_down)
     flat_grads = direction.reshape(matrix_count, head_size * head_size)
-    total = lax.psum(flat_grads, "ctx")
+    total = attach_leaves(flat_grads)
     norm_sizes = jnp.sqrt(jnp.sum(total * total, axis=1, keepdims=True))
     scaled = (total / (norm_sizes + 1e-06)).astype(jnp.bfloat16)
     iterate = scaled.reshape(matrix_count, head_size, head_size)

time: 237 us -> 648 us (2.73)
  waiting for transfers between devices: 117 us -> 527 us
  between operations: 15 us -> 1.64 us
  other arithmetic: 17.2 us -> 26.5 us
  starting transfers between devices: 0.04 us -> 7.83 us
    ppermute x0 -> x4, waiting for transfers between devices: none -> 527 us  [boxes_name(): side_arr = side_arr + ppermute(side_arr, mesh_ax, plain(1 << dev_j))]
    psum x1 -> x0, waiting for transfers between devices: 117 us -> none  [per_device(): total = lax.psum(flat_grads, 'ctx')]
    ppermute x0 -> x4, starting transfers between devices: none -> 7.83 us  [boxes_name(): side_arr = side_arr + ppermute(side_arr, mesh_ax, plain(1 << dev_j))]
    add x0 -> x3, other arithmetic: none -> 7.5 us  [boxes_name(): side_arr = side_arr + ppermute(side_arr, mesh_ax, plain(1 << dev_j))]
  transfers between devices with their start and end apart: 1 -> 4, of which waited for: 1 -> 4; matrix products, arithmetic and copies ran while one was open for 10% -> 3% of each run, Pallas kernels for 0% -> 0%
where the time goes in v1:
time: 648 us; the launch traced here: 647 us
  waiting for transfers between devices  527 us (81%)
  matrix products  52.3 us (8%)
  local copies, waits for them, and re-layouts  31.9 us (5%)
  other arithmetic  26.5 us (4%)
  starting transfers between devices  7.83 us (1%)
    ppermute x4, waiting for transfers between devices, boxes_name(): side_arr = side_arr + ppermute(side_arr, mesh_ax, plain(1 << dev_j))  527 us
    dot_general x3, matrix products, per_device(): jnp.einsum('mij,mjk->mik', polynomial, iterate, preferred_element_type=jn...  27.7 us
    unnamed x42, local copies, waits for them, and re-layouts  13.4 us
  transfers between devices with their start and end apart: 4, of which 4 were waited for; matrix products, arithmetic and copies ran while one was open for 3% of the time, Pallas kernels for 0%

profile of v1, /device:TPU:0, one launch (start us, length us, event | category | flops | bytes accessed | tf_op | source)
XLA Modules:
  0.0 647.5 jit_solution(11645522770556598835)
XLA Ops:
  0.6 0.0 copy-start.10
  0.6 0.0 copy-start.16
  0.7 0.0 copy-start.8
  0.7 0.0 copy-start.17
  0.7 1.8 fusion.41
  2.5 0.0 copy-done.10
  2.5 1.4 fusion.43
  3.9 0.0 copy-done.16
  3.9 0.1 convert_element_type.148
  4.0 0.5 fusion.61
  4.5 0.0 copy-start.15
  4.5 0.7 convolution_bitcast_fusion
  5.2 0.4 copy-done.15
  5.6 0.6 convolution_bitcast_fusion.2
  6.2 0.6 convolution_bitcast_fusion.1
  6.8 3.3 pad_maximum_fusion
  10.1 6.7 %copy.60 = f32[3,8,256,256]{3,1,2,0:T(8,128)} copy(f32[3,8,256,256]{2,3,1,0:T(8,128)} %pad_maximum_fusion) | data formatting | bytes 12582912
  16.8 0.5 collective-permute-start
  17.3 10.0 %collective-permute-done = f32[24,65536]{1,0:T(8,128)S(1)} collective-permute-done((f32[24,65536]{1,0:T(8,128)}, f32[24,65536]{1,0:T(8,128)S(1)}, u32[]{:S(2)}, u32[]{:S(2)}) %collective-permute-start) | collective-permute-done | bytes 6291488 | tf_op jit(solution)/shard_map/ppermute | solution.py:19
  27.3 3.6 add.73
  30.9 2.9 collective-permute-start.1
  33.8 135.8 %collective-permute-done.1 = f32[24,65536]{1,0:T(8,128)S(1)} collective-permute-done((f32[24,65536]{1,0:T(8,128)S(1)}, f32[24,65536]{1,0:T(8,128)S(1)}, u32[]{:S(2)}, u32[]{:S(2)}) %collective-permute-start.1) | collective-permute-done | bytes 6291488 | tf_op jit(solution)/shard_map/ppermute | solution.py:19
  169.7 0.6 add.74
  170.3 0.0 copy-start.6
  170.3 0.0 copy-start.11
  170.3 1.9 collective-permute-start.2
  172.2 135.2 %collective-permute-done.2 = f32[24,65536]{1,0:T(8,128)S(1)} collective-permute-done((f32[24,65536]{1,0:T(8,128)S(1)}, f32[24,65536]{1,0:T(8,128)S(1)}, u32[]{:S(2)}, u32[]{:S(2)}) %collective-permute-start.2) | collective-permute-done | bytes 6291488 | tf_op jit(solution)/shard_map/ppermute | solution.py:19
  307.4 3.3 add.75
  310.6 2.5 collective-permute-start.3
  313.2 0.5 copy.31
  313.7 0.5 copy.32
  314.2 0.0 copy-start.2
  314.3 1.9 copy.33
  316.1 0.0 copy-start.4
  316.1 3.1 maximum_convert_fusion
  319.2 6.5 %copy.45 = f32[3,8,256,256]{3,2,1,0:T(8,128)} copy(f32[3,8,256,256]{2,3,1,0:T(8,128)} %maximum_convert_fusion) | data formatting | bytes 12582912 | tf_op jit(solution)/shard_map/convert_element_type | solution.py:95
  325.8 1.0 multiply_reduce_fusion
  326.8 0.0 copy-start.9
  326.8 0.0 copy-start.12
  326.8 2.4 copy.56
  329.9 1.7 fusion.47
  331.6 2.5 fusion.29
  334.0 1.3 copy.30
  335.4 1.0 copy.49
  336.4 246.4 %collective-permute-done.3 = f32[24,65536]{1,0:T(8,128)} collective-permute-done((f32[24,65536]{1,0:T(8,128)}, f32[24,65536]{1,0:T(8,128)}, u32[]{:S(2)}, u32[]{:S(2)}) %collective-permute-start.3) | collective-permute-done | bytes 6291488 | tf_op jit(solution)/shard_map/ppermute | solution.py:19
  582.8 5.4 multiply_reduce_fusion.1
  588.2 0.4 divide_convert_fusion.1
  588.6 0.7 copy.61
  589.4 2.7 fusion.74
  592.0 7.8 %add_convert_fusion.4 = bf16[24,256,256]{2,1,0:T(8,128)(2,1)} fusion(bf16[24,256,256]{2,1,0:T(8,128)(2,1)S(1)} %bitcast.116, bf16[24,256,256]{2,1,0:T(8,128)(2,1)} %fusion.74), kind=kOutput, calls=%fused_computation.10 | convolution fusion | flops 1624768512 | bytes 9437184 | tf_op jit(solution)/shard_map/mij,mjk->mik/dot_general | solution.py:91
  599.9 5.5 fusion.75
  605.4 8.1 %add_convert_fusion.2 = bf16[24,256,256]{2,1,0:T(8,128)(2,1)S(1)} fusion(bf16[24,256,256]{2,1,0:T(8,128)(2,1)} %add_convert_fusion.4, bf16[24,256,256]{2,1,0:T(8,128)(2,1)} %fusion.75), kind=kOutput, calls=%fused_computation.8 | convolution fusion | flops 1624768512 | bytes 9437184 | tf_op jit(solution)/shard_map/mij,mjk->mik/dot_general | solution.py:91
  613.6 2.7 fusion.76
  616.2 11.7 %fusion.1 = (f32[24,256]{1,0:T(8,128)S(1)}, f32[24,256,256]{2,1,0:T(8,128)}) fusion(f32[3,8,256,256]{3,2,1,0:T(8,128)} %copy.45, bf16[24,256,256]{2,1,0:T(8,128)(2,1)S(1)} %add_convert_fusion.2, bf16[24,256,256]{2,1,0:T(8,128)(2,1)} %fusion.76), kind=kOutput, calls=%fused_computation.3 | convolution fusion | flops 1631053824 | bytes 18898944 | tf_op jit(solution)/shard_map/mij,mjk->mik/dot_general | solution.py:91
  628.0 6.7 %copy.44 = f32[3,8,256,256]{2,3,1,0:T(8,128)} copy(f32[3,8,256,256]{3,2,1,0:T(8,128)} %bitcast.129) | data formatting | bytes 12582912 | tf_op jit(solution)/shard_map/convert_element_type | solution.py:96
  634.7 0.0 copy-start.13
  634.7 4.6 divide_convert_fusion
  639.3 0.0 copy-start.14
  639.3 1.6 copy-done.7
  640.9 0.0 copy-done.13
  640.9 0.4 fusion.31
  641.4 3.5 convolution_convert_fusion
  644.9 1.5 copy.48
  646.4 1.1 broadcast_select_fusion
  (22 shorter events, 0.1 us)
Async XLA Ops:
  0.6 1.9 copy-start.10
  0.6 3.2 copy-start.16
  0.7 3.4 copy-start.8
  0.7 3.4 copy-start.17
  4.5 1.0 copy-start.15
  16.8 10.5 %collective-permute-start = (f32[24,65536]{1,0:T(8,128)}, f32[24,65536]{1,0:T(8,128)S(1)}, u32[]{:S(2)}, u32[]{:S(2)}) collective-permute-start(f32[24,65536]{1,0:T(8,128)} %bitcast.117), channel_id=1, source_target_pairs={{0,1},{1,0},{2,3},{3,2},{4,5},{5,4},{6,7},{7,6},{8,9},{9,8},{10,11... | collective-permute-start | bytes 18874376 | tf_op jit(solution)/shard_map/ppermute | solution.py:19
  30.9 138.8 %collective-permute-start.1 = (f32[24,65536]{1,0:T(8,128)S(1)}, f32[24,65536]{1,0:T(8,128)S(1)}, u32[]{:S(2)}, u32[]{:S(2)}) collective-permute-start(f32[24,65536]{1,0:T(8,128)S(1)} %add.73), channel_id=1, source_target_pairs={{0,2},{1,3},{2,0},{3,1},{4,6},{5,7},{6,4},{7,5},{8,10},{9,11},{10,... | collective-permute-start | bytes 18874376 | tf_op jit(solution)/shard_map/ppermute | solution.py:19
  170.3 142.9 %copy-start.6 = (bf16[8,256,256]{2,1,0:T(8,128)(2,1)S(1)}, bf16[8,256,256]{2,1,0:T(8,128)(2,1)}, u32[]{:S(2)}) copy-start(bf16[8,256,256]{2,1,0:T(8,128)(2,1)} %param.13) | copy-start | bytes 3145732
  170.3 143.4 %copy-start.11 = (bf16[8,256,256]{2,1,0:T(8,128)(2,1)S(1)}, bf16[8,256,256]{2,1,0:T(8,128)(2,1)}, u32[]{:S(2)}) copy-start(bf16[8,256,256]{2,1,0:T(8,128)(2,1)} %param.14) | copy-start | bytes 3145732
  170.3 137.0 %collective-permute-start.2 = (f32[24,65536]{1,0:T(8,128)S(1)}, f32[24,65536]{1,0:T(8,128)S(1)}, u32[]{:S(2)}, u32[]{:S(2)}) collective-permute-start(f32[24,65536]{1,0:T(8,128)S(1)} %add.74), channel_id=1, source_target_pairs={{0,4},{1,5},{2,6},{3,7},{4,0},{5,1},{6,2},{7,3},{8,12},{9,13},{10,... | collective-permute-start | bytes 18874376 | tf_op jit(solution)/shard_map/ppermute | solution.py:19
  310.6 272.2 %collective-permute-start.3 = (f32[24,65536]{1,0:T(8,128)}, f32[24,65536]{1,0:T(8,128)}, u32[]{:S(2)}, u32[]{:S(2)}) collective-permute-start(f32[24,65536]{1,0:T(8,128)} %add.75), channel_id=1, source_target_pairs={{0,8},{1,9},{2,10},{3,11},{4,12},{5,13},{6,14},{7,15},{8,0},{9,1},... | collective-permute-start | bytes 18874376 | tf_op jit(solution)/shard_map/ppermute | solution.py:19
  313.7 12.0 %copy-start = (bf16[8,256,256]{1,2,0:T(8,128)(2,1)}, bf16[8,256,256]{1,2,0:T(8,128)(2,1)S(1)}, u32[]{:S(2)}) copy-start(bf16[8,256,256]{1,2,0:T(8,128)(2,1)S(1)} %copy.31) | copy-start | bytes 3145732
  314.2 11.5 %copy-start.2 = (bf16[8,256,256]{1,2,0:T(8,128)(2,1)}, bf16[8,256,256]{1,2,0:T(8,128)(2,1)S(1)}, u32[]{:S(2)}) copy-start(bf16[8,256,256]{1,2,0:T(8,128)(2,1)S(1)} %copy.32) | copy-start | bytes 3145732
  316.1 9.6 %copy-start.4 = (bf16[8,256,256]{1,2,0:T(8,128)(2,1)}, bf16[8,256,256]{1,2,0:T(8,128)(2,1)S(1)}, u32[]{:S(2)}) copy-start(bf16[8,256,256]{1,2,0:T(8,128)(2,1)S(1)} %copy.33) | copy-start | bytes 3145732
  326.8 4.8 copy-start.9
  326.8 4.8 copy-start.12
  627.9 6.7 %copy-start.1 = (bf16[8,256,256]{1,2,0:T(8,128)(2,1)S(1)}, bf16[8,256,256]{1,2,0:T(8,128)(2,1)}, u32[]{:S(2)}) copy-start(bf16[8,256,256]{1,2,0:T(8,128)(2,1)} %copy-done) | copy-start | bytes 3145732
  627.9 6.7 %copy-start.3 = (bf16[8,256,256]{1,2,0:T(8,128)(2,1)S(1)}, bf16[8,256,256]{1,2,0:T(8,128)(2,1)}, u32[]{:S(2)}) copy-start(bf16[8,256,256]{1,2,0:T(8,128)(2,1)} %copy-done.2) | copy-start | bytes 3145732
  627.9 6.7 %copy-start.5 = (bf16[8,256,256]{1,2,0:T(8,128)(2,1)S(1)}, bf16[8,256,256]{1,2,0:T(8,128)(2,1)}, u32[]{:S(2)}) copy-start(bf16[8,256,256]{1,2,0:T(8,128)(2,1)} %copy-done.4) | copy-start | bytes 3145732
  634.7 6.2 copy-start.13
  639.3 1.6 copy-start.7
  639.3 2.1 copy-start.14
